TPU v7x, 32 devices: a whole 2x2x4 slice. The times are simulated.
32 devices in a mesh: rows: 8 (over z, y), cols: 4 (over x, core).
Axes of the slice: x: 2, y: 2, z: 4, core: 2. Of those that a mesh axis runs over, the one named last changes fastest.
Arguments:
- points: float32 [8192, 1024], P('rows', 'cols'), may hold values from -6 to 6
- pivots: int32 [2, 512], replicated, may hold values from 0 to 8191, as said below
- targets: float32 [8192, 256], P('rows', 'cols'), may hold values from -6 to 6
Outputs:
- factor: float32 [8192, 1024], P(('rows', 'cols'))
- projection: float32 [1024, 256], P(None, 'cols')
Inputs may be any that keep to these rules, and one draw needn't show every extreme that they name: All 1024 indices of both blocks are distinct. The points of one index of rows (an aligned run of 1024 indices) hold at most 512 pivots of the two blocks together, and in every draw some index of rows holds exactly 512.
All inputs are finite; a program needn't handle non-finite values.
Results may differ from a plain program's by a relative error of at most 0.0003.
Values sent between devices are 32-bit elements; how exact they have to be, the bound alone decides.
No kernel may reach another device: no remote copies, remote signals or barrier semaphores. Data moves between devices by JAX's collectives and lax.ppermute only.
A program may use at most 64 MiB of HBM per device.

v0:
```python
import math
import jax
import jax.numpy as jnp
from jax import lax
from jax.sharding import PartitionSpec as P

E = 1024
RIDGE = 0.001


def right_side_solve(low, values):
    return lax.linalg.triangular_solve(low, values, left_side=False, lower=True, transpose_a=True)


def shards(points, pivots, targets):
    highest = lax.Precision.HIGHEST
    rows_dev = points.shape[0]
    nrows = lax.axis_size("rows")
    row_me = lax.axis_index("rows")
    block = pivots.shape[1]
    flat = pivots.reshape(-1)
    owner = flat // rows_dev
    inside = flat - owner * rows_dev
    mine = owner == row_me
    capacity = min(rows_dev, 8 * block // nrows)
    hits = (owner[:, None] == jnp.arange(nrows, dtype=jnp.int32)[None, :]).astype(jnp.int32)
    before = jnp.cumsum(hits, axis=0) - hits
    slot = jnp.sum(before * hits, axis=1)
    place = jnp.where(mine, slot, capacity)
    slot_rows = jnp.zeros((capacity,), jnp.int32).at[place].set(inside, mode="drop")
    picked = points[slot_rows]
    gathered = lax.all_gather(picked, "rows", axis=0, tiled=True)
    pivot_part = gathered[owner * capacity + slot]
    own_rows = lax.all_to_all(points, "cols", split_axis=0, concat_axis=1, tiled=True)
    pivot_full = lax.all_gather(pivot_part, "cols", axis=1, tiled=True)
    own_norms = jnp.sum(own_rows * own_rows, axis=1)
    full_norms = jnp.sum(pivot_full * pivot_full, axis=1)
    cross = jnp.dot(own_rows, pivot_full.T, precision=highest, preferred_element_type=jnp.float32)
    dist = own_norms[:, None] + full_norms[None, :] - 2.0 * cross
    kern = jnp.exp(-dist / (2.0 * E))
    first = kern[:, :block]
    second = kern[:, block:]
    identity = jnp.eye(block, dtype=jnp.float32)
    every_norms = jnp.sum(pivot_full * pivot_full, axis=1)
    pivot_cross = jnp.dot(
        pivot_full, pivot_full.T, precision=highest, preferred_element_type=jnp.float32
    )
    pivot_kern = jnp.exp(
        -(every_norms[:, None] + every_norms[None, :] - 2.0 * pivot_cross) / (2.0 * E)
    )
    low_one = jnp.linalg.cholesky(pivot_kern[:block, :block] + RIDGE * identity)
    factor_one = right_side_solve(low_one, first)
    crossed = right_side_solve(low_one, pivot_kern[block:, :block])
    second_pivot = pivot_kern[block:, block:]
    resid = second - jnp.dot(
        factor_one, crossed.T, precision=highest, preferred_element_type=jnp.float32
    )
    schur = second_pivot - jnp.dot(
        crossed, crossed.T, precision=highest, preferred_element_type=jnp.float32
    )
    low_two = jnp.linalg.cholesky(schur + RIDGE * identity)
    second_lower_matrix = right_side_solve(low_two, resid)
    factor = jnp.concatenate([factor_one, second_lower_matrix], axis=1)
    scaling = 1.0 / math.sqrt(rows_dev * nrows)
    summed = lax.dot_general(
        lax.all_gather(factor, "cols", axis=0, tiled=True),
        targets,
        (((0,), (0,)), ((), ())),
        precision=highest,
        preferred_element_type=jnp.float32,
    )
    projection = lax.psum(summed, "rows") * scaling
    return (factor, projection)


def solution(mesh):
    return jax.shard_map(
        shards,
        mesh=mesh,
        in_specs=(P("rows", "cols"), P(), P("rows", "cols")),
        out_specs=(P(("rows", "cols"), None), P(None, "cols")),
        check_vma=False,
    )
```

profile of v0, /device:TPU:0, one launch (start us, length us, event | category | flops | bytes accessed | tf_op | source)
XLA Modules:
  0.0 580.4 jit_solution(16799073077159931661)
XLA Ops:
  12.3 4.3 scatter_custom_fusion
  16.6 3.5 gather_fusion
  20.1 75.6 %all-gather.8.cloned.1.call-done = f32[4096,256]{1,0:T(8,128)} async-done(((f32[512,256]{1,0:T(8,128)}), f32[4096,256]{1,0:T(8,128)}) %all-gather.8.cloned.1.call-update) | async-done | bytes 4194320 | tf_op jit(solution)/shard_map/all_gather | solution.py:32
  95.8 6.9 %gather_fusion.1 = f32[1024,256]{1,0:T(8,128)} fusion(f32[4096,256]{1,0:T(8,128)} %all-gather.8.cloned.1.call-done, s32[1024]{0:T(1024)S(1)} %broadcast_clamp_fusion), kind=kCustom, calls=%fused_computation.1 | custom fusion | bytes 2101248 | tf_op jit(solution)/shard_map/gather | solution.py:33
  102.7 3.5 all-to-all-start
  106.4 23.6 %all-to-all-done = f32[4,256,256]{2,1,0:T(8,128)S(1)} async-done(((f32[4,256,256]{2,1,0:T(8,128)}), f32[4,256,256]{2,1,0:T(8,128)S(1)}, u32[]{:S(2)}, u32[]{:S(2)}) %all-to-all-start) | async-done | bytes 1048608 | tf_op jit(solution)/shard_map/all_to_all | solution.py:34
  130.5 14.2 %all-gather.10.cloned.1.call-done = f32[1024,1024]{1,0:T(8,128)} async-done(((f32[1024,256]{1,0:T(8,128)}), f32[1024,1024]{1,0:T(8,128)}) %all-gather.10.cloned.1.call-update) | async-done | bytes 4194320 | tf_op jit(solution)/shard_map/all_gather | solution.py:35
  144.7 2.7 multiply_reduce_fusion
  148.1 14.4 %multiply_exponential_fusion = f32[1024,1024]{0,1:T(8,128)S(1)} fusion(f32[1024,1024]{1,0:T(8,128)S(1)} %copy-done.1, f32[1024]{0:T(1024)S(1)} %multiply_reduce_fusion), kind=kOutput, calls=%fused_computation.7 | convolution fusion | flops 12890144768 | bytes 8392704 | tf_op jit(solution)/shard_map/dot_general | solution.py:45
  166.4 11.7 %cholesky.286 = f32[128,128]{1,0:T(8,128)S(1)} custom-call(f32[128,128]{1,0:T(8,128)S(1)} %cholesky.426), custom_call_target="Cholesky" | custom-call | tf_op jit(solution)/shard_map/jit(cholesky)/cholesky | solution.py:51
  178.2 9.8 %custom-call.31 = f32[1,128,128]{1,2,0:T(8,128)S(1)} custom-call(f32[1,128,128]{2,1,0:T(8,128)S(1)} %get-tuple-element.95), custom_call_target="InvertDiagBlocksLowerTriangular" | custom-call | tf_op jit(solution)/shard_map/jit(cholesky)/cholesky | solution.py:51
  188.9 12.1 %cholesky.305 = f32[128,128]{1,0:T(8,128)S(1)} custom-call(f32[128,128]{1,0:T(8,128)S(1)} %cholesky.430), custom_call_target="Cholesky" | custom-call | tf_op jit(solution)/shard_map/jit(cholesky)/cholesky | solution.py:51
  201.1 9.8 %custom-call.32 = f32[1,128,128]{1,2,0:T(8,128)S(1)} custom-call(f32[1,128,128]{2,1,0:T(8,128)S(1)} %get-tuple-element.93), custom_call_target="InvertDiagBlocksLowerTriangular" | custom-call | tf_op jit(solution)/shard_map/jit(cholesky)/cholesky | solution.py:51
  212.9 11.7 %cholesky.326 = f32[128,128]{1,0:T(8,128)S(1)} custom-call(f32[128,128]{1,0:T(8,128)S(1)} %cholesky.435), custom_call_target="Cholesky" | custom-call | tf_op jit(solution)/shard_map/jit(cholesky)/cholesky | solution.py:51
  224.8 9.8 %custom-call.33 = f32[1,128,128]{1,2,0:T(8,128)S(1)} custom-call(f32[1,128,128]{2,1,0:T(8,128)S(1)} %get-tuple-element.91), custom_call_target="InvertDiagBlocksLowerTriangular" | custom-call | tf_op jit(solution)/shard_map/jit(cholesky)/cholesky | solution.py:51
  236.2 11.9 %cholesky.343 = f32[128,128]{1,0:T(8,128)S(1)} custom-call(f32[128,128]{1,0:T(8,128)S(1)} %convolution_subtract_fusion.16), custom_call_target="Cholesky" | custom-call | tf_op jit(solution)/shard_map/jit(cholesky)/cholesky | solution.py:51
  252.9 8.4 %while.5 = (s32[]{:T(128)}, f32[512,512]{0,1:T(8,128)S(1)}, s32[4,2]{0,1:T(2,128)S(1)}, f32[4,128,128]{2,1,0:T(8,128)S(1)}, s32[]{:T(128)}) while((s32[]{:T(128)}, f32[512,512]{0,1:T(8,128)S(1)}, s32[4,2]{0,1:T(2,128)S(1)}, f32[4,128,128]{2,1,0:T(8,128)S(1)}, s32[]{:T(128)}) %tuple.65), condition=%wide.while_cond, body=%wide.while_body.sunk | while | flops 2 | bytes 393329 | solution.py:12
  261.3 39.3 %custom-call.34 = f32[4,128,128]{1,2,0:T(8,128)S(1)} custom-call(f32[4,128,128]{2,1,0:T(8,128)S(1)} %get-tuple-element.26), custom_call_target="InvertDiagBlocksLowerTriangular" | custom-call | tf_op jit(solution)/shard_map/triangular_solve/custom-call.3 | solution.py:12
  302.0 5.5 fusion.4
  315.8 3.1 select_add_fusion
  322.2 12.1 %cholesky.358 = f32[128,128]{1,0:T(8,128)S(1)} custom-call(f32[128,128]{1,0:T(8,128)S(1)} %cholesky.439), custom_call_target="Cholesky" | custom-call | tf_op jit(solution)/shard_map/jit(cholesky)/cholesky | solution.py:61
  335.0 9.8 %custom-call.35 = f32[1,128,128]{1,2,0:T(8,128)S(1)} custom-call(f32[1,128,128]{2,1,0:T(8,128)S(1)} %get-tuple-element.89), custom_call_target="InvertDiagBlocksLowerTriangular" | custom-call | tf_op jit(solution)/shard_map/jit(cholesky)/cholesky | solution.py:61
  345.6 11.7 %cholesky.377 = f32[128,128]{1,0:T(8,128)S(1)} custom-call(f32[128,128]{1,0:T(8,128)S(1)} %cholesky.443), custom_call_target="Cholesky" | custom-call | tf_op jit(solution)/shard_map/jit(cholesky)/cholesky | solution.py:61
  358.1 9.8 %custom-call.36 = f32[1,128,128]{1,2,0:T(8,128)S(1)} custom-call(f32[1,128,128]{2,1,0:T(8,128)S(1)} %get-tuple-element.86), custom_call_target="InvertDiagBlocksLowerTriangular" | custom-call | tf_op jit(solution)/shard_map/jit(cholesky)/cholesky | solution.py:61
  368.6 11.9 %cholesky.398 = f32[128,128]{1,0:T(8,128)S(1)} custom-call(f32[128,128]{1,0:T(8,128)S(1)} %cholesky.448), custom_call_target="Cholesky" | custom-call | tf_op jit(solution)/shard_map/jit(cholesky)/cholesky | solution.py:61
  381.2 9.8 %custom-call.37 = f32[1,128,128]{1,2,0:T(8,128)S(1)} custom-call(f32[1,128,128]{2,1,0:T(8,128)S(1)} %get-tuple-element.83), custom_call_target="InvertDiagBlocksLowerTriangular" | custom-call | tf_op jit(solution)/shard_map/jit(cholesky)/cholesky | solution.py:61
  391.6 11.7 %cholesky.415 = f32[128,128]{1,0:T(8,128)S(1)} custom-call(f32[128,128]{1,0:T(8,128)S(1)} %convolution_subtract_fusion.15), custom_call_target="Cholesky" | custom-call | tf_op jit(solution)/shard_map/jit(cholesky)/cholesky | solution.py:61
  406.7 8.2 %while.6 = (s32[]{:T(128)}, f32[512,512]{1,0:T(8,128)S(1)}, s32[4,2]{0,1:T(2,128)S(1)}, f32[4,128,128]{2,1,0:T(8,128)S(1)}, s32[]{:T(128)}) while((s32[]{:T(128)}, f32[512,512]{1,0:T(8,128)S(1)}, s32[4,2]{0,1:T(2,128)S(1)}, f32[4,128,128]{2,1,0:T(8,128)S(1)}, s32[]{:T(128)}) %tuple.79), condition=%wide.while_cond.clone, body=%wide.while_body.clone.sunk | while | flops 2 | bytes 131189 | solution.py:12
  414.9 39.5 %custom-call.38 = f32[4,128,128]{1,2,0:T(8,128)S(1)} custom-call(f32[4,128,128]{2,1,0:T(8,128)S(1)} %get-tuple-element.27), custom_call_target="InvertDiagBlocksLowerTriangular" | custom-call | tf_op jit(solution)/shard_map/triangular_solve/custom-call.3 | solution.py:12
  461.5 32.2 %all-gather.6.cloned.1.call-done = f32[1024,1024]{0,1:T(8,128)} async-done(((f32[256,1024]{0,1:T(8,128)}), f32[1024,1024]{0,1:T(8,128)}) %all-gather.6.cloned.1.call-update) | async-done | bytes 4194320 | tf_op jit(solution)/shard_map/all_gather | solution.py:66
  493.7 7.0 %fusion.104 = f32[1024,64]{0,1:T(8,128)} fusion(f32[1024,1024]{0,1:T(8,128)} %all-gather.6.cloned.1.call-done, f32[1024,64]{0,1:T(8,128)S(1)} %copy-done), kind=kOutput, calls=%fused_computation.215 | convolution fusion | flops 805306368 | bytes 4718592 | tf_op jit(solution)/shard_map/dot_general | solution.py:65
  502.0 69.9 %all-reduce.3.cloned.1.call-done = f32[1024,64]{0,1:T(8,128)} async-done(((f32[1024,64]{0,1:T(8,128)}), f32[1024,64]{0,1:T(8,128)}) %all-reduce.3.cloned.1.call-update) | async-done | bytes 262160 | tf_op jit(solution)/shard_map/psum | solution.py:72
  (160 shorter events, 61.5 us)
Async XLA Ops:
  7.2 486.5 %copy-start = (f32[1024,64]{0,1:T(8,128)S(1)}, f32[1024,64]{0,1:T(8,128)}, u32[]{:S(2)}) copy-start(f32[1024,64]{0,1:T(8,128)} %param.8) | copy-start | bytes 786436
  7.2 88.6 %all-gather.8.cloned.1.call-start = ((), (), s32[]{:S(2)}) async-start(), calls=%async_computation.3 | async-start | bytes 4718592 | tf_op jit(solution)/shard_map/all_gather | solution.py:32
  20.1 124.6 %all-gather.10.cloned.1.call-start = ((), (), s32[]{:S(2)}) async-start(), calls=%async_computation.4 | async-start | bytes 5242880 | tf_op jit(solution)/shard_map/all_gather | solution.py:35
  102.7 27.3 %all-to-all-start = ((f32[4,256,256]{2,1,0:T(8,128)}), f32[4,256,256]{2,1,0:T(8,128)S(1)}, u32[]{:S(2)}, u32[]{:S(2)}) async-start(f32[4,256,256]{2,1,0:T(8,128)} %bitcast.12), calls=%async_computation | async-start | bytes 2097152 | tf_op jit(solution)/shard_map/all_to_all | solution.py:34
  106.2 387.5 %all-gather.6.cloned.1.call-start = ((), (), s32[]{:S(2)}) async-start(), calls=%async_computation.1 | async-start | bytes 5242880 | tf_op jit(solution)/shard_map/all_gather | solution.py:66
  144.7 3.4 copy-start.1
  162.5 1.9 copy-start.4
  166.4 34.7 %copy-start.3 = (f32[512,512]{1,0:T(8,128)}, f32[512,512]{1,0:T(8,128)S(1)}, u32[]{:S(2)}) copy-start(f32[512,512]{1,0:T(8,128)S(1)} %fusion.6) | copy-start | bytes 3145732
  308.5 10.5 %copy-start.5 = (f32[256,128]{0,1:T(8,128)}, f32[256,128]{0,1:T(8,128)S(1)}, u32[]{:S(2)}) copy-start(f32[256,128]{0,1:T(8,128)S(1)} %fusion.77) | copy-start | bytes 393220
  309.2 9.8 %copy-start.7 = (f32[256,128]{0,1:T(8,128)}, f32[256,128]{0,1:T(8,128)S(1)}, u32[]{:S(2)}) copy-start(f32[256,128]{0,1:T(8,128)S(1)} %fusion.79) | copy-start | bytes 393220
  310.1 8.9 %copy-start.9 = (f32[256,128]{0,1:T(8,128)}, f32[256,128]{0,1:T(8,128)S(1)}, u32[]{:S(2)}) copy-start(f32[256,128]{0,1:T(8,128)S(1)} %fusion.81) | copy-start | bytes 393220
  367.9 92.4 %copy-start.6 = (f32[256,128]{0,1:T(8,128)S(1)}, f32[256,128]{0,1:T(8,128)}, u32[]{:S(2)}) copy-start(f32[256,128]{0,1:T(8,128)} %copy-done.5) | copy-start | bytes 393220
  367.9 92.4 %copy-start.8 = (f32[256,128]{0,1:T(8,128)S(1)}, f32[256,128]{0,1:T(8,128)}, u32[]{:S(2)}) copy-start(f32[256,128]{0,1:T(8,128)} %copy-done.7) | copy-start | bytes 393220
  367.9 92.4 %copy-start.10 = (f32[256,128]{0,1:T(8,128)S(1)}, f32[256,128]{0,1:T(8,128)}, u32[]{:S(2)}) copy-start(f32[256,128]{0,1:T(8,128)} %copy-done.9) | copy-start | bytes 393220
  461.4 39.3 %copy-start.2 = (f32[256,1024]{0,1:T(8,128)S(1)}, f32[256,1024]{0,1:T(8,128)}, u32[]{:S(2)}) copy-start(f32[256,1024]{0,1:T(8,128)} %maximum_maximum_fusion) | copy-start | bytes 3145732
  461.4 110.5 %all-reduce.3.cloned.1.call-start = ((), (), s32[]{:S(2)}) async-start(), calls=%async_computation.2 | async-start | bytes 524288 | tf_op jit(solution)/shard_map/psum | solution.py:72
Sparse Core Ops, SparseCore 0:
  20.2 75.5 all-gather.7
  102.8 41.8 all-gather.9
  461.5 32.0 all-gather.5
  500.8 71.0 all-reduce.2
where the time goes:
time: 584 us; the launch traced here: 580 us
  other arithmetic  248 us (42%)
  waiting for transfers between devices  216 us (37%)
  matrix products  54.1 us (9%)
  local copies, waits for them, and re-layouts  39.3 us (7%)
  between operations  19.8 us (3%)
    another operation x15, other arithmetic, shards(): low_two = jnp.linalg.cholesky(schur + RIDGE * identity)  79.6 us
    another operation x5, other arithmetic, right_side_solve(): lax.linalg.triangular_solve(low, values, left_side=False, lower=True, tra...  79.1 us
    another operation x14, other arithmetic, shards(): low_one = jnp.linalg.cholesky(pivot_kern[:block, :block] + RIDGE * identity)  78.9 us
    all_gather x1, waiting for transfers between devices, shards(): gathered = lax.all_gather(picked, 'rows', axis=0, tiled=True)  75.6 us
    psum x1, waiting for transfers between devices, shards(): projection = lax.psum(summed, 'rows') * scaling  69.9 us
    all_gather x1, waiting for transfers between devices, shards(): lax.all_gather(factor, 'cols', axis=0, tiled=True)  32.2 us
    all_to_all x1, waiting for transfers between devices, shards(): lax.all_to_all(points, 'cols', split_axis=0, concat_axis=1, tiled=True)  23.6 us
    another operation x35, local copies, waits for them, and re-layouts, right_side_solve(): lax.linalg.triangular_solve(low, values, left_side=False, lower=True, tra...  16.4 us
  transfers between devices with their start and end apart: 5, of which 5 were waited for; matrix products, arithmetic and copies ran while one was open for 0% of the time, Pallas kernels for 0%

commit v1 on v0

--- a/solution.py
+++ b/solution.py
@@ -69,7 +69,7 @@
         precision=highest,
         preferred_element_type=jnp.float32,
     )
-    projection = lax.psum(summed, "rows") * scaling
+    projection = jnp.sum(lax.all_gather(summed, "rows"), axis=0) * scaling
     return (factor, projection)
 
 

time: 584 us -> 564 us (0.966)
  waiting for transfers between devices: 216 us -> 194 us
    psum x1 -> x0, waiting for transfers between devices: 69.9 us -> none  [shards(): projection = lax.psum(summed, 'rows') * scaling]
    all_gather x0 -> x1, waiting for transfers between devices: none -> 47.9 us  [shards(): projection = jnp.sum(lax.all_gather(summed, 'rows'), axis=0) * scaling]
where the time goes in v1:
time: 564 us; the launch traced here: 561 us
  other arithmetic  247 us (44%)
  waiting for transfers between devices  194 us (34%)
  matrix products  54.1 us (10%)
  local copies, waits for them, and re-layouts  42 us (7%)
  between operations  19.8 us (4%)
    another operation x15, other arithmetic, shards(): low_two = jnp.linalg.cholesky(schur + RIDGE * identity)  79.6 us
    another operation x5, other arithmetic, right_side_solve(): lax.linalg.triangular_solve(low, values, left_side=False, lower=True, tra...  79.1 us
    another operation x14, other arithmetic, shards(): low_one = jnp.linalg.cholesky(pivot_kern[:block, :block] + RIDGE * identity)  78.9 us
    all_gather x1, waiting for transfers between devices, shards(): gathered = lax.all_gather(picked, 'rows', axis=0, tiled=True)  75.6 us
    all_gather x1, waiting for transfers between devices, shards(): projection = jnp.sum(lax.all_gather(summed, 'rows'), axis=0) * scaling  47.9 us
    all_gather x1, waiting for transfers between devices, shards(): lax.all_gather(factor, 'cols', axis=0, tiled=True)  32.2 us
    all_to_all x1, waiting for transfers between devices, shards(): lax.all_to_all(points, 'cols', split_axis=0, concat_axis=1, tiled=True)  23.6 us
    another operation x35, local copies, waits for them, and re-layouts, right_side_solve(): lax.linalg.triangular_solve(low, values, left_side=False, lower=True, tra...  16.4 us
  transfers between devices with their start and end apart: 5, of which 5 were waited for; matrix products, arithmetic and copies ran while one was open for 0% of the time, Pallas kernels for 0%

profile of v1, /device:TPU:0, one launch (start us, length us, event | category | flops | bytes accessed | tf_op | source)
XLA Modules:
  0.0 560.7 jit_solution(11174036652650207555)
XLA Ops:
  12.3 4.3 scatter_custom_fusion
  16.6 3.5 gather_fusion
  20.1 75.6 %all-gather.10.cloned.1.call-done = f32[4096,256]{1,0:T(8,128)} async-done(((f32[512,256]{1,0:T(8,128)}), f32[4096,256]{1,0:T(8,128)}) %all-gather.10.cloned.1.call-update) | async-done | bytes 4194320 | tf_op jit(solution)/shard_map/all_gather | solution.py:32
  95.8 6.9 %gather_fusion.1 = f32[1024,256]{1,0:T(8,128)} fusion(f32[4096,256]{1,0:T(8,128)} %all-gather.10.cloned.1.call-done, s32[1024]{0:T(1024)S(1)} %broadcast_clamp_fusion), kind=kCustom, calls=%fused_computation.1 | custom fusion | bytes 2101248 | tf_op jit(solution)/shard_map/gather | solution.py:33
  102.7 3.5 all-to-all-start
  106.4 23.6 %all-to-all-done = f32[4,256,256]{2,1,0:T(8,128)S(1)} async-done(((f32[4,256,256]{2,1,0:T(8,128)}), f32[4,256,256]{2,1,0:T(8,128)S(1)}, u32[]{:S(2)}, u32[]{:S(2)}) %all-to-all-start) | async-done | bytes 1048608 | tf_op jit(solution)/shard_map/all_to_all | solution.py:34
  130.5 14.2 %all-gather.12.cloned.1.call-done = f32[1024,1024]{1,0:T(8,128)} async-done(((f32[1024,256]{1,0:T(8,128)}), f32[1024,1024]{1,0:T(8,128)}) %all-gather.12.cloned.1.call-update) | async-done | bytes 4194320 | tf_op jit(solution)/shard_map/all_gather | solution.py:35
  148.1 14.4 %multiply_exponential_fusion = f32[1024,1024]{0,1:T(8,128)S(1)} fusion(f32[1024,1024]{1,0:T(8,128)S(1)} %copy-done.1, f32[1024]{0:T(1024)S(1)} %multiply_reduce_fusion), kind=kOutput, calls=%fused_computation.7 | convolution fusion | flops 12890144768 | bytes 8392704 | tf_op jit(solution)/shard_map/dot_general | solution.py:45
  166.4 11.7 %cholesky.286 = f32[128,128]{1,0:T(8,128)S(1)} custom-call(f32[128,128]{1,0:T(8,128)S(1)} %cholesky.426), custom_call_target="Cholesky" | custom-call | tf_op jit(solution)/shard_map/jit(cholesky)/cholesky | solution.py:51
  178.2 9.8 %custom-call.31 = f32[1,128,128]{1,2,0:T(8,128)S(1)} custom-call(f32[1,128,128]{2,1,0:T(8,128)S(1)} %get-tuple-element.95), custom_call_target="InvertDiagBlocksLowerTriangular" | custom-call | tf_op jit(solution)/shard_map/jit(cholesky)/cholesky | solution.py:51
  188.9 12.1 %cholesky.305 = f32[128,128]{1,0:T(8,128)S(1)} custom-call(f32[128,128]{1,0:T(8,128)S(1)} %cholesky.430), custom_call_target="Cholesky" | custom-call | tf_op jit(solution)/shard_map/jit(cholesky)/cholesky | solution.py:51
  201.1 9.8 %custom-call.32 = f32[1,128,128]{1,2,0:T(8,128)S(1)} custom-call(f32[1,128,128]{2,1,0:T(8,128)S(1)} %get-tuple-element.93), custom_call_target="InvertDiagBlocksLowerTriangular" | custom-call | tf_op jit(solution)/shard_map/jit(cholesky)/cholesky | solution.py:51
  212.9 11.7 %cholesky.326 = f32[128,128]{1,0:T(8,128)S(1)} custom-call(f32[128,128]{1,0:T(8,128)S(1)} %cholesky.435), custom_call_target="Cholesky" | custom-call | tf_op jit(solution)/shard_map/jit(cholesky)/cholesky | solution.py:51
  224.8 9.8 %custom-call.33 = f32[1,128,128]{1,2,0:T(8,128)S(1)} custom-call(f32[1,128,128]{2,1,0:T(8,128)S(1)} %get-tuple-element.91), custom_call_target="InvertDiagBlocksLowerTriangular" | custom-call | tf_op jit(solution)/shard_map/jit(cholesky)/cholesky | solution.py:51
  236.2 11.9 %cholesky.343 = f32[128,128]{1,0:T(8,128)S(1)} custom-call(f32[128,128]{1,0:T(8,128)S(1)} %convolution_subtract_fusion.16), custom_call_target="Cholesky" | custom-call | tf_op jit(solution)/shard_map/jit(cholesky)/cholesky | solution.py:51
  252.9 8.4 %while.5 = (s32[]{:T(128)}, f32[512,512]{0,1:T(8,128)S(1)}, s32[4,2]{0,1:T(2,128)S(1)}, f32[4,128,128]{2,1,0:T(8,128)S(1)}, s32[]{:T(128)}) while((s32[]{:T(128)}, f32[512,512]{0,1:T(8,128)S(1)}, s32[4,2]{0,1:T(2,128)S(1)}, f32[4,128,128]{2,1,0:T(8,128)S(1)}, s32[]{:T(128)}) %tuple.65), condition=%wide.while_cond, body=%wide.while_body.sunk | while | flops 2 | bytes 393329 | solution.py:12
  261.3 39.3 %custom-call.34 = f32[4,128,128]{1,2,0:T(8,128)S(1)} custom-call(f32[4,128,128]{2,1,0:T(8,128)S(1)} %get-tuple-element.26), custom_call_target="InvertDiagBlocksLowerTriangular" | custom-call | tf_op jit(solution)/shard_map/triangular_solve/custom-call.3 | solution.py:12
  302.0 5.5 fusion.4
  315.8 3.1 select_add_fusion
  322.2 12.1 %cholesky.358 = f32[128,128]{1,0:T(8,128)S(1)} custom-call(f32[128,128]{1,0:T(8,128)S(1)} %cholesky.439), custom_call_target="Cholesky" | custom-call | tf_op jit(solution)/shard_map/jit(cholesky)/cholesky | solution.py:61
  335.0 9.8 %custom-call.35 = f32[1,128,128]{1,2,0:T(8,128)S(1)} custom-call(f32[1,128,128]{2,1,0:T(8,128)S(1)} %get-tuple-element.89), custom_call_target="InvertDiagBlocksLowerTriangular" | custom-call | tf_op jit(solution)/shard_map/jit(cholesky)/cholesky | solution.py:61
  345.6 11.7 %cholesky.377 = f32[128,128]{1,0:T(8,128)S(1)} custom-call(f32[128,128]{1,0:T(8,128)S(1)} %cholesky.443), custom_call_target="Cholesky" | custom-call | tf_op jit(solution)/shard_map/jit(cholesky)/cholesky | solution.py:61
  358.1 9.8 %custom-call.36 = f32[1,128,128]{1,2,0:T(8,128)S(1)} custom-call(f32[1,128,128]{2,1,0:T(8,128)S(1)} %get-tuple-element.86), custom_call_target="InvertDiagBlocksLowerTriangular" | custom-call | tf_op jit(solution)/shard_map/jit(cholesky)/cholesky | solution.py:61
  368.6 11.9 %cholesky.398 = f32[128,128]{1,0:T(8,128)S(1)} custom-call(f32[128,128]{1,0:T(8,128)S(1)} %cholesky.448), custom_call_target="Cholesky" | custom-call | tf_op jit(solution)/shard_map/jit(cholesky)/cholesky | solution.py:61
  381.2 9.8 %custom-call.37 = f32[1,128,128]{1,2,0:T(8,128)S(1)} custom-call(f32[1,128,128]{2,1,0:T(8,128)S(1)} %get-tuple-element.83), custom_call_target="InvertDiagBlocksLowerTriangular" | custom-call | tf_op jit(solution)/shard_map/jit(cholesky)/cholesky | solution.py:61
  391.6 11.7 %cholesky.415 = f32[128,128]{1,0:T(8,128)S(1)} custom-call(f32[128,128]{1,0:T(8,128)S(1)} %convolution_subtract_fusion.15), custom_call_target="Cholesky" | custom-call | tf_op jit(solution)/shard_map/jit(cholesky)/cholesky | solution.py:61
  406.7 8.2 %while.6 = (s32[]{:T(128)}, f32[512,512]{1,0:T(8,128)S(1)}, s32[4,2]{0,1:T(2,128)S(1)}, f32[4,128,128]{2,1,0:T(8,128)S(1)}, s32[]{:T(128)}) while((s32[]{:T(128)}, f32[512,512]{1,0:T(8,128)S(1)}, s32[4,2]{0,1:T(2,128)S(1)}, f32[4,128,128]{2,1,0:T(8,128)S(1)}, s32[]{:T(128)}) %tuple.79), condition=%wide.while_cond.clone, body=%wide.while_body.clone.sunk | while | flops 2 | bytes 131189 | solution.py:12
  414.9 39.5 %custom-call.38 = f32[4,128,128]{1,2,0:T(8,128)S(1)} custom-call(f32[4,128,128]{2,1,0:T(8,128)S(1)} %get-tuple-element.27), custom_call_target="InvertDiagBlocksLowerTriangular" | custom-call | tf_op jit(solution)/shard_map/triangular_solve/custom-call.3 | solution.py:12
  461.5 32.2 %all-gather.8.cloned.1.call-done = f32[1024,1024]{0,1:T(8,128)} async-done(((f32[256,1024]{0,1:T(8,128)}), f32[1024,1024]{0,1:T(8,128)}) %all-gather.8.cloned.1.call-update) | async-done | bytes 4194320 | tf_op jit(solution)/shard_map/all_gather | solution.py:66
  493.7 7.0 %fusion.104 = f32[1024,64]{0,1:T(8,128)} fusion(f32[1024,1024]{0,1:T(8,128)} %all-gather.8.cloned.1.call-done, f32[1024,64]{0,1:T(8,128)S(1)} %copy-done), kind=kOutput, calls=%fused_computation.216 | convolution fusion | flops 805306368 | bytes 4718592 | tf_op jit(solution)/shard_map/dot_general | solution.py:65
  502.0 47.9 %all-gather.14.cloned.1.call-done = f32[8192,64]{0,1:T(8,128)} async-done(((f32[1024,64]{0,1:T(8,128)}), f32[8192,64]{0,1:T(8,128)}) %all-gather.14.cloned.1.call-update) | async-done | bytes 2097168 | tf_op jit(solution)/shard_map/all_gather | solution.py:72
  549.9 2.8 copy.78
  (162 shorter events, 63.8 us)
Async XLA Ops:
  7.2 486.5 %copy-start = (f32[1024,64]{0,1:T(8,128)S(1)}, f32[1024,64]{0,1:T(8,128)}, u32[]{:S(2)}) copy-start(f32[1024,64]{0,1:T(8,128)} %param.8) | copy-start | bytes 786436
  7.2 88.6 %all-gather.10.cloned.1.call-start = ((), (), s32[]{:S(2)}) async-start(), calls=%async_computation.2 | async-start | bytes 4718592 | tf_op jit(solution)/shard_map/all_gather | solution.py:32
  20.1 124.6 %all-gather.12.cloned.1.call-start = ((), (), s32[]{:S(2)}) async-start(), calls=%async_computation.3 | async-start | bytes 5242880 | tf_op jit(solution)/shard_map/all_gather | solution.py:35
  102.7 27.3 %all-to-all-start = ((f32[4,256,256]{2,1,0:T(8,128)}), f32[4,256,256]{2,1,0:T(8,128)S(1)}, u32[]{:S(2)}, u32[]{:S(2)}) async-start(f32[4,256,256]{2,1,0:T(8,128)} %bitcast.12), calls=%async_computation | async-start | bytes 2097152 | tf_op jit(solution)/shard_map/all_to_all | solution.py:34
  106.2 387.5 %all-gather.8.cloned.1.call-start = ((), (), s32[]{:S(2)}) async-start(), calls=%async_computation.1 | async-start | bytes 5242880 | tf_op jit(solution)/shard_map/all_gather | solution.py:66
  144.7 3.4 copy-start.1
  162.5 1.9 copy-start.4
  166.4 34.7 %copy-start.3 = (f32[512,512]{1,0:T(8,128)}, f32[512,512]{1,0:T(8,128)S(1)}, u32[]{:S(2)}) copy-start(f32[512,512]{1,0:T(8,128)S(1)} %fusion.6) | copy-start | bytes 3145732
  308.5 10.5 %copy-start.5 = (f32[256,128]{0,1:T(8,128)}, f32[256,128]{0,1:T(8,128)S(1)}, u32[]{:S(2)}) copy-start(f32[256,128]{0,1:T(8,128)S(1)} %fusion.77) | copy-start | bytes 393220
  309.2 9.8 %copy-start.7 = (f32[256,128]{0,1:T(8,128)}, f32[256,128]{0,1:T(8,128)S(1)}, u32[]{:S(2)}) copy-start(f32[256,128]{0,1:T(8,128)S(1)} %fusion.79) | copy-start | bytes 393220
  310.1 8.9 %copy-start.9 = (f32[256,128]{0,1:T(8,128)}, f32[256,128]{0,1:T(8,128)S(1)}, u32[]{:S(2)}) copy-start(f32[256,128]{0,1:T(8,128)S(1)} %fusion.81) | copy-start | bytes 393220
  367.9 92.4 %copy-start.6 = (f32[256,128]{0,1:T(8,128)S(1)}, f32[256,128]{0,1:T(8,128)}, u32[]{:S(2)}) copy-start(f32[256,128]{0,1:T(8,128)} %copy-done.5) | copy-start | bytes 393220
  367.9 92.4 %copy-start.8 = (f32[256,128]{0,1:T(8,128)S(1)}, f32[256,128]{0,1:T(8,128)}, u32[]{:S(2)}) copy-start(f32[256,128]{0,1:T(8,128)} %copy-done.7) | copy-start | bytes 393220
  367.9 92.4 %copy-start.10 = (f32[256,128]{0,1:T(8,128)S(1)}, f32[256,128]{0,1:T(8,128)}, u32[]{:S(2)}) copy-start(f32[256,128]{0,1:T(8,128)} %copy-done.9) | copy-start | bytes 393220
  461.4 39.3 %copy-start.2 = (f32[256,1024]{0,1:T(8,128)S(1)}, f32[256,1024]{0,1:T(8,128)}, u32[]{:S(2)}) copy-start(f32[256,1024]{0,1:T(8,128)} %maximum_maximum_fusion) | copy-start | bytes 3145732
  461.4 88.5 %all-gather.14.cloned.1.call-start = ((), (), s32[]{:S(2)}) async-start(), calls=%async_computation.4 | async-start | bytes 2359296 | tf_op jit(solution)/shard_map/all_gather | solution.py:72
Sparse Core Ops, SparseCore 0:
  20.2 75.5 all-gather.9
  102.8 41.8 all-gather.11
  461.5 32.0 all-gather.7
  500.8 49.0 all-gather.13
